TPU v7x, 32 devices: a whole 2x2x4 slice. The times are simulated.
32 devices in a mesh: groups: 2 (over x), pass: 2 (over core), mp: 8 (over z, y).
Axes of the slice: x: 2, y: 2, z: 4, core: 2. Of those that a mesh axis runs over, the one named last changes fastest.
Arguments:
- passages: bfloat16 [4096, 1024], P(('groups', 'pass', 'mp')), parts along dimension 0, may hold values from -6 to 6
- gain: float32 [1024], replicated, may hold values from 0.1 to 1.9
- w_in: bfloat16 [1024, 65536], P(None, 'mp'), may hold values from -0.1875 to 0.1875
- w_out: bfloat16 [65536, 1024], P('mp'), may hold values from -0.0234375 to 0.0234375
- w_key: bfloat16 [1024, 16384], P(None, 'mp'), may hold values from -0.1875 to 0.1875
- w_value: bfloat16 [1024, 16384], P(None, 'mp'), may hold values from -0.1875 to 0.1875
- queries: bfloat16 [32, 256, 16384], P(('groups', 'pass'), None, 'mp'), parts along dimension 0, may hold values from -72 to 72
- ids: int32 [4096], P('groups'), parts along dimension 0, may hold values from 0 to 4094, as said below
- counts: int32 [32], P(('groups', 'pass')), parts along dimension 0, may hold values from 1 to 255, as said below
Outputs:
- context: bfloat16 [32, 256, 16384], P(('groups', 'pass'), None, 'mp'), parts along dimension 0
There are 2 independent parts, one for each index of `groups`. A program takes and returns all parts, laid end to end along the dimension named above; an argument that names none is the same for every part. Nothing has to cross between parts.
Inputs may be any that keep to these rules, and one draw needn't show every extreme that they name: counts sum to 2048; the last question has exactly 255 passages and some question exactly 1. ids are distinct; ids[r] // 256 is a question q with ids[r] % 256 < counts[q], and every such slot is named by exactly one row.
All inputs are finite; a program needn't handle non-finite values.
Results may differ from a plain program's by a relative error of at most 0.02.
The roundings to bfloat16 on the way count: a program that leaves them out, or rounds other values in their place, can miss the bound.
Values may be sent and summed in bfloat16 or wider, within the bound.
A program may use at most 192 MiB of HBM per device.

v0:
```python
import jax
import jax.numpy as jnp
from jax import lax
from jax.sharding import PartitionSpec as P

HEAD = 128
QUERIES = 256
SLOTS = 256


def feed_forward(row_block, gain, w_in, w_out):
    wide = row_block.astype(jnp.float32)
    scale = lax.rsqrt(jnp.mean(wide * wide, axis=-1, keepdims=True) + 1e-06)
    normed = (wide * scale * gain).astype(jnp.bfloat16)
    hidden = jax.nn.relu(jnp.dot(normed, w_in, preferred_element_type=jnp.float32)).astype(
        jnp.bfloat16
    )
    return jnp.dot(hidden, w_out, preferred_element_type=jnp.float32)


def per_device(passages, gain, w_in, w_out, w_key, w_value, queries, ids, counts):
    gathered = lax.all_gather(passages, "mp", axis=0, tiled=True)
    own_share = lax.psum_scatter(
        feed_forward(gathered, gain, w_in, w_out), "mp", scatter_dimension=0, tiled=True
    )
    own_rows = (passages.astype(jnp.float32) + own_share).astype(jnp.bfloat16)
    encoded = lax.all_gather(own_rows, "mp", axis=0, tiled=True)
    local_questions = counts.shape[0]
    model_width = passages.shape[1]
    slot_total = local_questions * SLOTS
    all_rows = lax.all_gather(encoded, "pass", axis=0, tiled=True)
    shifted = ids - lax.axis_index("pass") * slot_total
    inside = (shifted >= 0) & (shifted < slot_total)
    target = jnp.where(inside, shifted, slot_total)
    slot_rows = (
        jnp.zeros((slot_total, model_width), jnp.bfloat16).at[target].set(all_rows, mode="drop")
    )
    key_rows = jnp.dot(slot_rows, w_key, preferred_element_type=jnp.float32).astype(jnp.bfloat16)
    value_rows = jnp.dot(slot_rows, w_value, preferred_element_type=jnp.float32).astype(
        jnp.bfloat16
    )
    local_heads = w_key.shape[1] // HEAD
    keyed = key_rows.reshape(local_questions, SLOTS, local_heads, HEAD)
    valued = value_rows.reshape(local_questions, SLOTS, local_heads, HEAD)
    asked = queries.reshape(local_questions, QUERIES, local_heads, HEAD)
    scores = jnp.einsum("qihd,qjhd->qhij", asked, keyed, preferred_element_type=jnp.float32)
    position = jnp.arange(SLOTS, dtype=jnp.int32)
    valid_key = position[None, None, None, :] < counts[:, None, None, None]
    scores = jnp.where(valid_key, scores, -1e30)
    peak = jnp.max(scores, axis=-1, keepdims=True)
    raised = jnp.where(valid_key, jnp.exp(scores - peak), 0.0)
    weights = (raised / jnp.sum(raised, axis=-1, keepdims=True)).astype(jnp.bfloat16)
    mixed = jnp.einsum("qhij,qjhd->qihd", weights, valued, preferred_element_type=jnp.float32)
    return mixed.reshape(local_questions, QUERIES, local_heads * HEAD).astype(jnp.bfloat16)


def solution(mesh):
    placed = (
        P(("groups", "pass", "mp"), None),
        P(),
        P(None, "mp"),
        P("mp", None),
        P(None, "mp"),
        P(None, "mp"),
        P(("groups", "pass"), None, "mp"),
        P("groups"),
        P(("groups", "pass")),
    )
    return jax.shard_map(
        per_device,
        mesh=mesh,
        in_specs=placed,
        out_specs=P(("groups", "pass"), None, "mp"),
        check_vma=False,
    )
```

profile of v0, /device:TPU:0, one launch (start us, length us, event | category | flops | bytes accessed | tf_op | source)
XLA Modules:
  0.0 415.7 jit_solution(15696875548011298462)
XLA Ops:
  6.5 0.7 all-gather.4.cloned.1.call-update
  7.3 0.0 reduce-scatter.2.cloned.1.call-start
  7.3 54.0 %all-gather.4.cloned.1.call-done = bf16[1024,1024]{1,0:T(8,128)(2,1)} async-done(((bf16[128,1024]{1,0:T(8,128)(2,1)}), bf16[1024,1024]{1,0:T(8,128)(2,1)}) %all-gather.4.cloned.1.call-update) | async-done | bytes 2097168 | tf_op jit(solution)/shard_map/all_gather | solution.py:22
  61.3 2.1 fusion.18
  63.4 26.8 %maximum_convert_fusion.clone.4 = bf16[1024,8192]{1,0:T(8,128)(2,1)} fusion(bf16[1024,8192]{1,0:T(8,128)(2,1)} %param.11, bf16[1024,1024]{1,0:T(8,128)(2,1)} %all-gather.4.cloned.1.call-done, f32[1024]{0:T(1024)} %param.10, f32[1024]{0:T(1024)S(1)} %add_rsqrt_fusion), kind=kOutput, calls=%fused_computation.8.clone.clone.clone.1 | convolution fusion | flops 17200840704 | bytes 35659776 | tf_op jit(solution)/shard_map/dot_general | solution.py:15
  90.2 23.6 %fusion.27 = f32[1024,1024]{1,0:T(8,128)} fusion(bf16[8192,1024]{1,0:T(8,128)(2,1)} %param.12, bf16[1024,8192]{1,0:T(8,128)(2,1)} %maximum_convert_fusion.clone.4), kind=kOutput, calls=%fused_computation.30 | convolution fusion | flops 17179869184 | bytes 37748736 | tf_op jit(solution)/shard_map/dot_general | solution.py:18
  113.8 0.0 reduce-scatter.2.cloned.1.call-update
  113.8 0.0 all-gather.6.cloned.1.call-start
  113.9 86.9 %reduce-scatter.2.cloned.1.call-done = f32[128,1024]{1,0:T(8,128)} async-done(((f32[1024,1024]{1,0:T(8,128)}), f32[128,1024]{1,0:T(8,128)}) %reduce-scatter.2.cloned.1.call-update) | async-done | bytes 524304 | tf_op jit(solution)/shard_map/reduce_scatter | solution.py:23
  200.8 1.8 add_convert_fusion
  202.6 0.0 all-gather.6.cloned.1.call-update
  202.6 0.0 all-gather.8.cloned.1.call-start
  202.7 49.0 %all-gather.6.cloned.1.call-done = bf16[1024,1024]{1,0:T(8,128)(2,1)} async-done(((bf16[128,1024]{1,0:T(8,128)(2,1)}), bf16[1024,1024]{1,0:T(8,128)(2,1)}) %all-gather.6.cloned.1.call-update) | async-done | bytes 2097168 | tf_op jit(solution)/shard_map/all_gather | solution.py:27
  251.7 0.1 iota_compare_fusion
  251.8 13.5 %all-gather.8.cloned.1.call-done = bf16[2048,1024]{1,0:T(8,128)(2,1)} async-done(((bf16[1024,1024]{1,0:T(8,128)(2,1)}), bf16[2048,1024]{1,0:T(8,128)(2,1)}) %all-gather.8.cloned.1.call-update) | async-done | bytes 4194320 | tf_op jit(solution)/shard_map/all_gather | solution.py:31
  265.3 13.0 %scatter_custom_fusion = bf16[2048,1024]{1,0:T(8,128)(2,1)} fusion(s32[2048]{0:T(1024)S(1)} %compare_select_fusion, bf16[2048,1024]{1,0:T(8,128)(2,1)} %all-gather.8.cloned.1.call-done, bf16[]{:T(256)} %constant.10.clone.1), kind=kCustom, calls=%fused_computation.28 | custom fusion | bytes 4194816 | tf_op jit(solution)/shard_map/scatter | solution.py:36
  278.3 13.9 %convert_bitcast_fusion = bf16[256,8,16,128]{3,1,2,0:T(8,128)(2,1)} fusion(bf16[2048,1024]{1,0:T(8,128)(2,1)} %scatter_custom_fusion, bf16[1024,2048]{1,0:T(8,128)(2,1)} %param.13), kind=kOutput, calls=%fused_computation.18 | convolution fusion | flops 8594128896 | bytes 16777216 | tf_op jit(solution)/shard_map/dot_general | solution.py:38
  292.3 9.9 %copy.18 = bf16[256,8,16,128]{3,2,1,0:T(8,128)(2,1)} copy(bf16[256,8,16,128]{3,1,2,0:T(8,128)(2,1)} %convert_bitcast_fusion) | data formatting | bytes 16777216
  302.2 13.0 %convert_bitcast_fusion.1 = bf16[256,8,16,128]{3,1,2,0:T(8,128)(2,1)} fusion(bf16[2048,1024]{1,0:T(8,128)(2,1)S(1)} %copy-done, bf16[1024,2048]{1,0:T(8,128)(2,1)} %param.14), kind=kOutput, calls=%fused_computation.19 | convolution fusion | flops 8594128896 | bytes 16777216 | tf_op jit(solution)/shard_map/dot_general | solution.py:39
  315.2 9.7 %copy.17 = bf16[256,8,16,128]{3,2,1,0:T(8,128)(2,1)} copy(bf16[256,8,16,128]{3,1,2,0:T(8,128)(2,1)} %convert_bitcast_fusion.1) | data formatting | bytes 16777216
  324.9 16.6 %fusion.10 = f32[8,16,256,256]{3,2,1,0:T(8,128)} fusion(bf16[8,256,16,128]{3,2,1,0:T(8,128)(2,1)} %bitcast.42, bf16[8,256,2048]{2,1,0:T(8,128)(2,1)} %param.15), kind=kOutput, calls=%fused_computation.13 | convolution fusion | flops 2147483648 | bytes 50331648 | tf_op jit(solution)/shard_map/qihd,qjhd->qhij/dot_general | solution.py:46
  341.5 37.7 %fusion.31 = (f32[8,16,256]{2,1,0:T(8,128)S(1)}, f32[8,16,256,256]{2,3,1,0:T(8,128)}) fusion(f32[8,16,256,256]{3,2,1,0:T(8,128)} %fusion.10, pred[8,256]{1,0:T(8,128)(4,1)S(1)} %iota_compare_fusion), kind=kOutput, calls=%fused_computation.37 | output fusion | flops 41943296 | bytes 67241984 | tf_op jit(solution)/shard_map/sub | solution.py:51
  379.2 18.6 %fusion.15 = bf16[8,16,128,256]{3,2,1,0:T(8,128)(2,1)} fusion(f32[8,16,256,256]{2,3,1,0:T(8,128)} %get-tuple-element.6, f32[8,16,256]{2,1,0:T(8,128)S(1)} %get-tuple-element.5, bf16[8,256,16,128]{3,2,1,0:T(8,128)(2,1)} %bitcast.43), kind=kOutput, calls=%fused_computation.20 | convolution fusion | flops 2168455168 | bytes 50462720 | tf_op jit(solution)/shard_map/qhij,qjhd->qihd/dot_general | solution.py:53
  397.8 11.4 %copy.14 = bf16[8,256,2048]{2,1,0:T(8,128)(2,1)} copy(bf16[8,256,2048]{1,2,0:T(8,128)(2,1)} %bitcast.44) | data formatting | bytes 16777216 | tf_op jit(solution)/shard_map/convert_element_type | solution.py:54
  (12 shorter events, 0.0 us)
Async XLA Ops:
  6.5 54.8 %all-gather.4.cloned.1.call-start = ((), (), s32[]{:S(2)}) async-start(), calls=%async_computation.1 | async-start | bytes 2359296 | tf_op jit(solution)/shard_map/all_gather | solution.py:22
  7.3 193.5 %reduce-scatter.2.cloned.1.call-start = ((), (), s32[]{:S(2)}) async-start(), calls=%async_computation.2 | async-start | bytes 4718592 | tf_op jit(solution)/shard_map/reduce_scatter | solution.py:23
  90.2 110.6 %copy-start.1 = (bf16[128,1024]{1,0:T(8,128)(2,1)S(1)}, bf16[128,1024]{1,0:T(8,128)(2,1)}, u32[]{:S(2)}) copy-start(bf16[128,1024]{1,0:T(8,128)(2,1)} %param.9) | copy-start | bytes 786436
  90.2 161.5 %copy-start.3 = (s32[8]{0:T(128)S(1)}, s32[8]{0:T(128)}, u32[]{:S(2)}) copy-start(s32[8]{0:T(128)} %param.17) | copy-start | bytes 100
  90.2 161.6 %copy-start.2 = (s32[2048]{0:T(1024)S(1)}, s32[2048]{0:T(1024)}, u32[]{:S(2)}) copy-start(s32[2048]{0:T(1024)} %param.16) | copy-start | bytes 24580
  113.8 137.9 %all-gather.6.cloned.1.call-start = ((), (), s32[]{:S(2)}) async-start(), calls=%async_computation.3 | async-start | bytes 2359296 | tf_op jit(solution)/shard_map/all_gather | solution.py:27
  202.6 62.7 %all-gather.8.cloned.1.call-start = ((), (), s32[]{:S(2)}) async-start(), calls=%async_computation.4 | async-start | bytes 6291456 | tf_op jit(solution)/shard_map/all_gather | solution.py:31
  292.3 9.9 %copy-start = (bf16[2048,1024]{1,0:T(8,128)(2,1)S(1)}, bf16[2048,1024]{1,0:T(8,128)(2,1)}, u32[]{:S(2)}) copy-start(bf16[2048,1024]{1,0:T(8,128)(2,1)} %scatter_custom_fusion) | copy-start | bytes 12582916
Sparse Core Ops, SparseCore 0:
  9.5 51.7 all-gather.3
  113.9 86.8 reduce-scatter.1
  202.9 48.7 all-gather.5
  253.1 12.1 all-gather.7
where the time goes:
time: 416 us
  waiting for transfers between devices  204 us (49%)
  matrix products  113 us (27%)
  local copies, waits for them, and re-layouts  44.1 us (11%)
  other arithmetic  41.6 us (10%)
  between operations  13.2 us (3%)
    reduce_scatter x1, waiting for transfers between devices, per_device(): lax.psum_scatter(feed_forward(gathered, gain, w_in, w_out), 'mp', scatter...  86.9 us
    all_gather x1, waiting for transfers between devices, per_device(): gathered = lax.all_gather(passages, 'mp', axis=0, tiled=True)  54 us
    all_gather x1, waiting for transfers between devices, per_device(): encoded = lax.all_gather(own_rows, 'mp', axis=0, tiled=True)  49 us
    sub x1, other arithmetic, per_device(): raised = jnp.where(valid_key, jnp.exp(scores - peak), 0.0)  37.7 us
    dot_general x1, matrix products, feed_forward(): jnp.dot(normed, w_in, preferred_element_type=jnp.float32)  26.8 us
    dot_general x1, matrix products, feed_forward(): return jnp.dot(hidden, w_out, preferred_element_type=jnp.float32)  23.6 us
    unnamed x10, local copies, waits for them, and re-layouts  19.7 us
    dot_general x1, matrix products, per_device(): jnp.einsum('qhij,qjhd->qihd', weights, valued, preferred_element_type=jnp...  18.6 us
  transfers between devices with their start and end apart: 4, of which 4 were waited for; matrix products, arithmetic and copies ran while one was open for 0% of the time, Pallas kernels for 0%

commit v1 on v0

--- a/solution.py
+++ b/solution.py
@@ -19,7 +19,14 @@
 
 
 def per_device(passages, gain, w_in, w_out, w_key, w_value, queries, ids, counts):
-    gathered = lax.all_gather(passages, "mp", axis=0, tiled=True)
+    ways = lax.axis_size("mp")
+    pieces = [passages]
+    for far in range(1, ways):
+        pieces.append(
+            lax.ppermute(pieces[far - 1], "mp", [(d, (d - 1) % ways) for d in range(ways)])
+        )
+    line = jnp.concatenate(pieces, axis=0)
+    gathered = jnp.roll(line, lax.axis_index("mp") * passages.shape[0], axis=0)
     own_share = lax.psum_scatter(
         feed_forward(gathered, gain, w_in, w_out), "mp", scatter_dimension=0, tiled=True
     )

time: 416 us -> 431 us (1.036)
  starting transfers between devices: 0.13 us -> 37.3 us
  waiting for transfers between devices: 204 us -> 183 us
    all_gather x1 -> x0, waiting for transfers between devices: 54 us -> none  [per_device(): gathered = lax.all_gather(passages, 'mp', axis=0, tiled=True)]
    ppermute x0 -> x7, starting transfers between devices: none -> 37 us  [per_device(): lax.ppermute(pieces[far - 1], 'mp', [(d, (d - 1) % ways) for d in range(w...]
    ppermute x0 -> x7, waiting for transfers between devices: none -> 30.1 us  [per_device(): lax.ppermute(pieces[far - 1], 'mp', [(d, (d - 1) % ways) for d in range(w...]
    unnamed x10 -> x27, local copies, waits for them, and re-layouts: 19.7 us -> 20.9 us
  transfers between devices with their start and end apart: 4 -> 10, of which waited for: 4 -> 10; matrix products, arithmetic and copies ran while one was open for 0% -> 0% of each run, Pallas kernels for 0% -> 0%
where the time goes in v1:
time: 431 us
  waiting for transfers between devices  183 us (42%)
  matrix products  112 us (26%)
  local copies, waits for them, and re-layouts  45.4 us (11%)
  other arithmetic  39.9 us (9%)
  starting transfers between devices  37.3 us (9%)
  between operations  13.3 us (3%)
    reduce_scatter x1, waiting for transfers between devices, per_device(): lax.psum_scatter(feed_forward(gathered, gain, w_in, w_out), 'mp', scatter...  90.3 us
    all_gather x1, waiting for transfers between devices, per_device(): encoded = lax.all_gather(own_rows, 'mp', axis=0, tiled=True)  48.8 us
    sub x1, other arithmetic, per_device(): raised = jnp.where(valid_key, jnp.exp(scores - peak), 0.0)  37.5 us
    ppermute x7, starting transfers between devices, per_device(): lax.ppermute(pieces[far - 1], 'mp', [(d, (d - 1) % ways) for d in range(w...  37 us
    ppermute x7, waiting for transfers between devices, per_device(): lax.ppermute(pieces[far - 1], 'mp', [(d, (d - 1) % ways) for d in range(w...  30.1 us
    dot_general x1, matrix products, feed_forward(): jnp.dot(normed, w_in, preferred_element_type=jnp.float32)  26.2 us
    dot_general x1, matrix products, feed_forward(): return jnp.dot(hidden, w_out, preferred_element_type=jnp.float32)  23.6 us
    unnamed x27, local copies, waits for them, and re-layouts  20.9 us
  transfers between devices with their start and end apart: 10, of which 10 were waited for; matrix products, arithmetic and copies ran while one was open for 0% of the time, Pallas kernels for 0%

profile of v1, /device:TPU:0, one launch (start us, length us, event | category | flops | bytes accessed | tf_op | source)
XLA Modules:
  0.0 430.6 jit_solution(6098051771919716740)
XLA Ops:
  6.5 6.0 %collective-permute-start = (bf16[128,1024]{1,0:T(8,128)(2,1)}, bf16[128,1024]{1,0:T(8,128)(2,1)S(1)}, u32[]{:S(2)}, u32[]{:S(2)}) collective-permute-start(bf16[128,1024]{1,0:T(8,128)(2,1)} %param.9), channel_id=1, source_target_pairs={{0,7},{1,0},{2,1},{3,2},{4,3},{5,4},{6,5},{7,6},{8,15},{9,8},{10,9... | collective-permute-start | bytes 786440 | tf_op jit(solution)/shard_map/ppermute | solution.py:26
  12.6 5.9 %collective-permute-done = bf16[128,1024]{1,0:T(8,128)(2,1)S(1)} collective-permute-done((bf16[128,1024]{1,0:T(8,128)(2,1)}, bf16[128,1024]{1,0:T(8,128)(2,1)S(1)}, u32[]{:S(2)}, u32[]{:S(2)}) %collective-permute-start) | collective-permute-done | bytes 262176 | tf_op jit(solution)/shard_map/ppermute | solution.py:26
  18.5 5.1 %collective-permute-start.1 = (bf16[128,1024]{1,0:T(8,128)(2,1)S(1)}, bf16[128,1024]{1,0:T(8,128)(2,1)S(1)}, u32[]{:S(2)}, u32[]{:S(2)}) collective-permute-start(bf16[128,1024]{1,0:T(8,128)(2,1)S(1)} %collective-permute-done), channel_id=1, source_target_pairs={{0,7},{1,0},{2,1},{3,2},{4,3},{5,4},{6,5},{7,6},{8,15},{9,8},{10,9... | collective-permute-start | bytes 786440 | tf_op jit(solution)/shard_map/ppermute | solution.py:26
  23.5 4.7 %collective-permute-done.1 = bf16[128,1024]{1,0:T(8,128)(2,1)S(1)} collective-permute-done((bf16[128,1024]{1,0:T(8,128)(2,1)S(1)}, bf16[128,1024]{1,0:T(8,128)(2,1)S(1)}, u32[]{:S(2)}, u32[]{:S(2)}) %collective-permute-start.1) | collective-permute-done | bytes 262176 | tf_op jit(solution)/shard_map/ppermute | solution.py:26
  28.2 5.2 %collective-permute-start.2 = (bf16[128,1024]{1,0:T(8,128)(2,1)S(1)}, bf16[128,1024]{1,0:T(8,128)(2,1)S(1)}, u32[]{:S(2)}, u32[]{:S(2)}) collective-permute-start(bf16[128,1024]{1,0:T(8,128)(2,1)S(1)} %collective-permute-done.1), channel_id=1, source_target_pairs={{0,7},{1,0},{2,1},{3,2},{4,3},{5,4},{6,5},{7,6},{8,15},{9,8},{10,9... | collective-permute-start | bytes 786440 | tf_op jit(solution)/shard_map/ppermute | solution.py:26
  37.3 5.2 %collective-permute-start.3 = (bf16[128,1024]{1,0:T(8,128)(2,1)S(1)}, bf16[128,1024]{1,0:T(8,128)(2,1)S(1)}, u32[]{:S(2)}, u32[]{:S(2)}) collective-permute-start(bf16[128,1024]{1,0:T(8,128)(2,1)S(1)} %collective-permute-done.2), channel_id=1, source_target_pairs={{0,7},{1,0},{2,1},{3,2},{4,3},{5,4},{6,5},{7,6},{8,15},{9,8},{10,9... | collective-permute-start | bytes 786440 | tf_op jit(solution)/shard_map/ppermute | solution.py:26
  46.4 5.2 %collective-permute-start.4 = (bf16[128,1024]{1,0:T(8,128)(2,1)S(1)}, bf16[128,1024]{1,0:T(8,128)(2,1)S(1)}, u32[]{:S(2)}, u32[]{:S(2)}) collective-permute-start(bf16[128,1024]{1,0:T(8,128)(2,1)S(1)} %collective-permute-done.3), channel_id=1, source_target_pairs={{0,7},{1,0},{2,1},{3,2},{4,3},{5,4},{6,5},{7,6},{8,15},{9,8},{10,9... | collective-permute-start | bytes 786440 | tf_op jit(solution)/shard_map/ppermute | solution.py:26
  55.4 5.2 %collective-permute-start.5 = (bf16[128,1024]{1,0:T(8,128)(2,1)S(1)}, bf16[128,1024]{1,0:T(8,128)(2,1)S(1)}, u32[]{:S(2)}, u32[]{:S(2)}) collective-permute-start(bf16[128,1024]{1,0:T(8,128)(2,1)S(1)} %collective-permute-done.4), channel_id=1, source_target_pairs={{0,7},{1,0},{2,1},{3,2},{4,3},{5,4},{6,5},{7,6},{8,15},{9,8},{10,9... | collective-permute-start | bytes 786440 | tf_op jit(solution)/shard_map/ppermute | solution.py:26
  60.7 5.0 %collective-permute-done.5 = bf16[128,1024]{1,0:T(8,128)(2,1)S(1)} collective-permute-done((bf16[128,1024]{1,0:T(8,128)(2,1)S(1)}, bf16[128,1024]{1,0:T(8,128)(2,1)S(1)}, u32[]{:S(2)}, u32[]{:S(2)}) %collective-permute-start.5) | collective-permute-done | bytes 262176 | tf_op jit(solution)/shard_map/ppermute | solution.py:26
  65.7 5.2 %collective-permute-start.6 = (bf16[128,1024]{1,0:T(8,128)(2,1)S(1)}, bf16[128,1024]{1,0:T(8,128)(2,1)S(1)}, u32[]{:S(2)}, u32[]{:S(2)}) collective-permute-start(bf16[128,1024]{1,0:T(8,128)(2,1)S(1)} %collective-permute-done.5), channel_id=1, source_target_pairs={{0,7},{1,0},{2,1},{3,2},{4,3},{5,4},{6,5},{7,6},{8,15},{9,8},{10,9... | collective-permute-start | bytes 786440 | tf_op jit(solution)/shard_map/ppermute | solution.py:26
  75.6 26.2 %fusion.56 = bf16[1024,8192]{1,0:T(8,128)(2,1)} fusion(bf16[1024,8192]{1,0:T(8,128)(2,1)} %param.11, f32[1024]{0:T(1024)S(1)} %copy-done.4, f32[1024]{0:T(1024)S(1)} %add_rsqrt_fusion, bf16[2048,1024]{1,0:T(8,128)(2,1)S(1)} %constant_dynamic-update-slice_fusion, s32[]{:T(128)S(6)} %select_n.33), kind=kOutput, calls=%bitcast_fusion.2.clone.1 | convolution fusion | flops 17200840704 | bytes 35659780 | tf_op jit(solution)/shard_map/dot_general | solution.py:15
  101.8 23.6 %fusion.30 = f32[1024,1024]{1,0:T(8,128)} fusion(bf16[8192,1024]{1,0:T(8,128)(2,1)} %param.12, bf16[1024,8192]{1,0:T(8,128)(2,1)} %fusion.56), kind=kOutput, calls=%fused_computation.54 | convolution fusion | flops 17179869184 | bytes 37748736 | tf_op jit(solution)/shard_map/dot_general | solution.py:18
  125.4 90.3 %reduce-scatter.2.cloned.1.call-done = f32[128,1024]{1,0:T(8,128)} async-done(((f32[1024,1024]{1,0:T(8,128)}), f32[128,1024]{1,0:T(8,128)}) %reduce-scatter.2.cloned.1.call-update) | async-done | bytes 524304 | tf_op jit(solution)/shard_map/reduce_scatter | solution.py:30
  217.7 48.8 %all-gather.3.cloned.1.call-done = bf16[1024,1024]{1,0:T(8,128)(2,1)} async-done(((bf16[128,1024]{1,0:T(8,128)(2,1)}), bf16[1024,1024]{1,0:T(8,128)(2,1)}) %all-gather.3.cloned.1.call-update) | async-done | bytes 2097168 | tf_op jit(solution)/shard_map/all_gather | solution.py:34
  266.7 13.7 %all-gather.5.cloned.1.call-done = bf16[2048,1024]{1,0:T(8,128)(2,1)} async-done(((bf16[1024,1024]{1,0:T(8,128)(2,1)}), bf16[2048,1024]{1,0:T(8,128)(2,1)}) %all-gather.5.cloned.1.call-update) | async-done | bytes 4194320 | tf_op jit(solution)/shard_map/all_gather | solution.py:38
  280.4 13.0 %scatter_custom_fusion = bf16[2048,1024]{1,0:T(8,128)(2,1)} fusion(s32[2048]{0:T(1024)S(1)} %compare_select_fusion, bf16[2048,1024]{1,0:T(8,128)(2,1)} %all-gather.5.cloned.1.call-done, bf16[]{:T(256)} %constant.23.clone.1), kind=kCustom, calls=%fused_computation.28 | custom fusion | bytes 4194816 | tf_op jit(solution)/shard_map/scatter | solution.py:43
  293.4 13.9 %convert_bitcast_fusion = bf16[256,8,16,128]{3,1,2,0:T(8,128)(2,1)} fusion(bf16[2048,1024]{1,0:T(8,128)(2,1)} %scatter_custom_fusion, bf16[1024,2048]{1,0:T(8,128)(2,1)} %param.13), kind=kOutput, calls=%fused_computation.18 | convolution fusion | flops 8594128896 | bytes 16777216 | tf_op jit(solution)/shard_map/dot_general | solution.py:45
  307.3 9.9 %copy.18 = bf16[256,8,16,128]{3,2,1,0:T(8,128)(2,1)} copy(bf16[256,8,16,128]{3,1,2,0:T(8,128)(2,1)} %convert_bitcast_fusion) | data formatting | bytes 16777216
  317.3 13.0 %convert_bitcast_fusion.1 = bf16[256,8,16,128]{3,1,2,0:T(8,128)(2,1)} fusion(bf16[2048,1024]{1,0:T(8,128)(2,1)S(1)} %copy-done, bf16[1024,2048]{1,0:T(8,128)(2,1)} %param.14), kind=kOutput, calls=%fused_computation.19 | convolution fusion | flops 8594128896 | bytes 16777216 | tf_op jit(solution)/shard_map/dot_general | solution.py:46
  330.3 9.8 %copy.17 = bf16[256,8,16,128]{3,2,1,0:T(8,128)(2,1)} copy(bf16[256,8,16,128]{3,1,2,0:T(8,128)(2,1)} %convert_bitcast_fusion.1) | data formatting | bytes 16777216
  340.0 16.5 %fusion.10 = f32[8,16,256,256]{3,2,1,0:T(8,128)} fusion(bf16[8,256,16,128]{3,2,1,0:T(8,128)(2,1)} %bitcast.50, bf16[8,256,2048]{2,1,0:T(8,128)(2,1)} %param.15), kind=kOutput, calls=%fused_computation.13 | convolution fusion | flops 2147483648 | bytes 50331648 | tf_op jit(solution)/shard_map/qihd,qjhd->qhij/dot_general | solution.py:53
  356.6 37.5 %fusion.29 = (f32[8,16,256]{2,1,0:T(8,128)S(1)}, f32[8,16,256,256]{2,3,1,0:T(8,128)}) fusion(f32[8,16,256,256]{3,2,1,0:T(8,128)} %fusion.10, pred[8,256]{1,0:T(8,128)(4,1)S(1)} %iota_compare_fusion), kind=kOutput, calls=%fused_computation.53 | output fusion | flops 41943296 | bytes 67241984 | tf_op jit(solution)/shard_map/sub | solution.py:58
  394.1 18.6 %fusion.15 = bf16[8,16,128,256]{3,2,1,0:T(8,128)(2,1)} fusion(f32[8,16,256,256]{2,3,1,0:T(8,128)} %get-tuple-element.6, f32[8,16,256]{2,1,0:T(8,128)S(1)} %get-tuple-element.5, bf16[8,256,16,128]{3,2,1,0:T(8,128)(2,1)} %bitcast.51), kind=kOutput, calls=%fused_computation.20 | convolution fusion | flops 2168455168 | bytes 50462720 | tf_op jit(solution)/shard_map/qhij,qjhd->qihd/dot_general | solution.py:60
  412.7 11.4 %copy.14 = bf16[8,256,2048]{2,1,0:T(8,128)(2,1)} copy(bf16[8,256,2048]{1,2,0:T(8,128)(2,1)} %bitcast.52) | data formatting | bytes 16777216 | tf_op jit(solution)/shard_map/convert_element_type | solution.py:61
  (41 shorter events, 18.5 us)
Async XLA Ops:
  6.5 68.3 %copy-start.1 = (bf16[128,1024]{1,0:T(8,128)(2,1)S(1)}, bf16[128,1024]{1,0:T(8,128)(2,1)}, u32[]{:S(2)}) copy-start(bf16[128,1024]{1,0:T(8,128)(2,1)} %param.9) | copy-start | bytes 786436
  6.5 209.2 %reduce-scatter.2.cloned.1.call-start = ((), (), s32[]{:S(2)}) async-start(), calls=%async_computation.1 | async-start | bytes 4718592 | tf_op jit(solution)/shard_map/reduce_scatter | solution.py:30
  6.5 11.9 %collective-permute-start = (bf16[128,1024]{1,0:T(8,128)(2,1)}, bf16[128,1024]{1,0:T(8,128)(2,1)S(1)}, u32[]{:S(2)}, u32[]{:S(2)}) collective-permute-start(bf16[128,1024]{1,0:T(8,128)(2,1)} %param.9), channel_id=1, source_target_pairs={{0,7},{1,0},{2,1},{3,2},{4,3},{5,4},{6,5},{7,6},{8,15},{9,8},{10,9... | collective-permute-start | bytes 786440 | tf_op jit(solution)/shard_map/ppermute | solution.py:26
  18.5 9.8 %collective-permute-start.1 = (bf16[128,1024]{1,0:T(8,128)(2,1)S(1)}, bf16[128,1024]{1,0:T(8,128)(2,1)S(1)}, u32[]{:S(2)}, u32[]{:S(2)}) collective-permute-start(bf16[128,1024]{1,0:T(8,128)(2,1)S(1)} %collective-permute-done), channel_id=1, source_target_pairs={{0,7},{1,0},{2,1},{3,2},{4,3},{5,4},{6,5},{7,6},{8,15},{9,8},{10,9... | collective-permute-start | bytes 786440 | tf_op jit(solution)/shard_map/ppermute | solution.py:26
  28.2 9.1 %collective-permute-start.2 = (bf16[128,1024]{1,0:T(8,128)(2,1)S(1)}, bf16[128,1024]{1,0:T(8,128)(2,1)S(1)}, u32[]{:S(2)}, u32[]{:S(2)}) collective-permute-start(bf16[128,1024]{1,0:T(8,128)(2,1)S(1)} %collective-permute-done.1), channel_id=1, source_target_pairs={{0,7},{1,0},{2,1},{3,2},{4,3},{5,4},{6,5},{7,6},{8,15},{9,8},{10,9... | collective-permute-start | bytes 786440 | tf_op jit(solution)/shard_map/ppermute | solution.py:26
  37.3 9.1 %collective-permute-start.3 = (bf16[128,1024]{1,0:T(8,128)(2,1)S(1)}, bf16[128,1024]{1,0:T(8,128)(2,1)S(1)}, u32[]{:S(2)}, u32[]{:S(2)}) collective-permute-start(bf16[128,1024]{1,0:T(8,128)(2,1)S(1)} %collective-permute-done.2), channel_id=1, source_target_pairs={{0,7},{1,0},{2,1},{3,2},{4,3},{5,4},{6,5},{7,6},{8,15},{9,8},{10,9... | collective-permute-start | bytes 786440 | tf_op jit(solution)/shard_map/ppermute | solution.py:26
  46.4 9.1 %collective-permute-start.4 = (bf16[128,1024]{1,0:T(8,128)(2,1)S(1)}, bf16[128,1024]{1,0:T(8,128)(2,1)S(1)}, u32[]{:S(2)}, u32[]{:S(2)}) collective-permute-start(bf16[128,1024]{1,0:T(8,128)(2,1)S(1)} %collective-permute-done.3), channel_id=1, source_target_pairs={{0,7},{1,0},{2,1},{3,2},{4,3},{5,4},{6,5},{7,6},{8,15},{9,8},{10,9... | collective-permute-start | bytes 786440 | tf_op jit(solution)/shard_map/ppermute | solution.py:26
  55.4 10.3 %collective-permute-start.5 = (bf16[128,1024]{1,0:T(8,128)(2,1)S(1)}, bf16[128,1024]{1,0:T(8,128)(2,1)S(1)}, u32[]{:S(2)}, u32[]{:S(2)}) collective-permute-start(bf16[128,1024]{1,0:T(8,128)(2,1)S(1)} %collective-permute-done.4), channel_id=1, source_target_pairs={{0,7},{1,0},{2,1},{3,2},{4,3},{5,4},{6,5},{7,6},{8,15},{9,8},{10,9... | collective-permute-start | bytes 786440 | tf_op jit(solution)/shard_map/ppermute | solution.py:26
  60.7 14.8 %copy-start.4 = (f32[1024]{0:T(1024)S(1)}, f32[1024]{0:T(1024)}, u32[]{:S(2)}) copy-start(f32[1024]{0:T(1024)} %param.10) | copy-start | bytes 12292
  65.7 9.1 %collective-permute-start.6 = (bf16[128,1024]{1,0:T(8,128)(2,1)S(1)}, bf16[128,1024]{1,0:T(8,128)(2,1)S(1)}, u32[]{:S(2)}, u32[]{:S(2)}) collective-permute-start(bf16[128,1024]{1,0:T(8,128)(2,1)S(1)} %collective-permute-done.5), channel_id=1, source_target_pairs={{0,7},{1,0},{2,1},{3,2},{4,3},{5,4},{6,5},{7,6},{8,15},{9,8},{10,9... | collective-permute-start | bytes 786440 | tf_op jit(solution)/shard_map/ppermute | solution.py:26
  125.4 141.2 %copy-start.3 = (s32[8]{0:T(128)S(1)}, s32[8]{0:T(128)}, u32[]{:S(2)}) copy-start(s32[8]{0:T(128)} %param.17) | copy-start | bytes 100
  125.4 141.3 %copy-start.2 = (s32[2048]{0:T(1024)S(1)}, s32[2048]{0:T(1024)}, u32[]{:S(2)}) copy-start(s32[2048]{0:T(1024)} %param.16) | copy-start | bytes 24580
  125.4 141.2 %all-gather.3.cloned.1.call-start = ((), (), s32[]{:S(2)}) async-start(), calls=%async_computation.2 | async-start | bytes 2359296 | tf_op jit(solution)/shard_map/all_gather | solution.py:34
  217.5 62.8 %all-gather.5.cloned.1.call-start = ((), (), s32[]{:S(2)}) async-start(), calls=%async_computation.3 | async-start | bytes 6291456 | tf_op jit(solution)/shard_map/all_gather | solution.py:38
  307.3 9.9 %copy-start = (bf16[2048,1024]{1,0:T(8,128)(2,1)S(1)}, bf16[2048,1024]{1,0:T(8,128)(2,1)}, u32[]{:S(2)}) copy-start(bf16[2048,1024]{1,0:T(8,128)(2,1)} %scatter_custom_fusion) | copy-start | bytes 12582916
Sparse Core Ops, SparseCore 0:
  125.5 90.1 reduce-scatter.1
  217.8 48.7 all-gather.2
  268.1 12.1 all-gather.4
